TPU v7x, 32 devices: a whole 2x2x4 slice. The times are simulated.
32 devices in a mesh: slab: 2 (over y), docs: 4 (over x, core), blk: 4 (over z).
Axes of the slice: x: 2, y: 2, z: 4, core: 2. Of those that a mesh axis runs over, the one named last changes fastest.
Arguments:
- pooled: bfloat16 [16384, 768], P(('slab', 'docs', 'blk')), parts along dimension 0, may hold values from -6 to 6
- proj_weight: bfloat16 [768, 768], replicated, may hold values from -0.21875 to 0.21875
- cluster: int32 [16384], P(('slab', 'docs', 'blk')), parts along dimension 0, may hold values from 0 to 143, as said below
Outputs:
- best_sim: float32 [16384], P(('slab', 'docs', 'blk')), parts along dimension 0
There are 2 independent parts, one for each index of `slab`. A program takes and returns all parts, laid end to end along the dimension named above; an argument that names none is the same for every part. Nothing has to cross between parts.
Inputs may be any that keep to these rules, and one draw needn't show every extreme that they name: Clusters below 16 are large, the others small. The documents of one device hold exactly 128 of large clusters and 384 of small ones. Among one device's documents at most 64 of large clusters share the value of cluster modulo the size of docs, and at most 48 of small clusters share the value of (cluster - 16) modulo the number of devices of docs and blk; in every draw one value of each kind holds exactly that many on every device.
All inputs are finite; a program needn't handle non-finite values.
Results may differ from a plain program's by a relative error of at most 0.0012.
Values may be sent and summed in bfloat16 or wider, within the bound.
A program may use at most 64 MiB of HBM per device.

v0:
```python
import jax
import jax.numpy as jnp
from jax import lax
from jax.sharding import PartitionSpec as P

BIG_OWN = 4


def passed_along(shard, axis, by):
    count = lax.axis_size(axis)
    return lax.ppermute(shard, axis, [(i, (i + by) % count) for i in range(count)])


def score_block(queries, others):
    return lax.dot_general(
        queries, others, (((1,), (1,)), ((), ())), preferred_element_type=jnp.float32
    )


def masked_max(queries, query_ids, others, other_ids, query_pos, other_pos):
    scores = score_block(queries, others)
    allowed = (
        (query_ids[:, None] == other_ids[None, :])
        & (query_ids[:, None] >= 0)
        & (query_pos[:, None] != other_pos[None, :])
    )
    return jnp.max(jnp.where(allowed, scores, -1.0), axis=1)


def body(pooled, proj_weight, cluster):
    shards = lax.axis_size("docs")
    blocks = lax.axis_size("blk")
    doc_rows = pooled.shape[0]
    feature = proj_weight.shape[1]
    big_count = doc_rows // 4
    small_count = doc_rows - big_count
    cap_big = 2 * big_count // shards
    cap_small = 2 * small_count // (shards * blocks)
    projected = jnp.dot(pooled, proj_weight, preferred_element_type=jnp.float32)
    embedded = (
        projected / jnp.sqrt(jnp.sum(projected * projected, axis=1, keepdims=True) + 1e-06)
    ).astype(jnp.bfloat16)
    large_limit = BIG_OWN * shards
    is_big = cluster < large_limit
    big_owner = cluster % shards
    small_target = (cluster - large_limit) % (shards * blocks)
    bucket = jnp.where(is_big, big_owner, shards + small_target)
    buckets = shards + shards * blocks
    onehot = (bucket[:, None] == jnp.arange(buckets, dtype=jnp.int32)[None, :]).astype(jnp.int32)
    before = jnp.cumsum(onehot, axis=0) - onehot
    slot_rank = jnp.sum(before * onehot, axis=1)
    big_slot = jnp.where(is_big, big_owner * cap_big + slot_rank, shards * cap_big)
    small_slot = jnp.where(
        is_big, shards * blocks * cap_small, small_target * cap_small + slot_rank
    )
    send_big = (
        jnp.zeros((shards * cap_big, feature), jnp.bfloat16)
        .at[big_slot]
        .set(embedded, mode="drop")
        .reshape(shards, cap_big, feature)
    )
    big_ids = (
        jnp.full((shards * cap_big,), -1, jnp.int32)
        .at[big_slot]
        .set(cluster, mode="drop")
        .reshape(shards, cap_big)
    )
    send_small = (
        jnp.zeros((shards * blocks * cap_small, feature), jnp.bfloat16)
        .at[small_slot]
        .set(embedded, mode="drop")
    )
    small_ids = (
        jnp.full((shards * blocks * cap_small,), -1, jnp.int32)
        .at[small_slot]
        .set(cluster, mode="drop")
    )
    got_big, got_big_ids = (
        lax.all_to_all(send_big, "docs", split_axis=0, concat_axis=0, tiled=True),
        lax.all_to_all(big_ids, "docs", split_axis=0, concat_axis=0, tiled=True),
    )
    group_mine = got_big.reshape(-1, feature)
    group_ids = got_big_ids.reshape(-1)
    group_count = group_mine.shape[0]
    got_small, got_small_ids = (
        lax.all_to_all(
            send_small.reshape(shards * blocks, cap_small, feature),
            ("docs", "blk"),
            split_axis=0,
            concat_axis=0,
            tiled=True,
        ),
        lax.all_to_all(
            small_ids.reshape(shards * blocks, cap_small),
            ("docs", "blk"),
            split_axis=0,
            concat_axis=0,
            tiled=True,
        ),
    )
    small_rows = got_small.reshape(-1, feature)
    small_row_ids = got_small_ids.reshape(-1)
    small_total = small_rows.shape[0]
    small_pos = jnp.arange(small_total, dtype=jnp.int32)
    block_size = min(512, small_total)
    small_parts = []
    for first_row in range(0, small_total, block_size):
        last_row = min(first_row + block_size, small_total)
        small_parts.append(
            masked_max(
                small_rows[first_row:last_row],
                small_row_ids[first_row:last_row],
                small_rows,
                small_row_ids,
                small_pos[first_row:last_row],
                small_pos,
            )
        )
    best_small = jnp.concatenate(small_parts)
    local_pos = jnp.arange(group_count, dtype=jnp.int32)
    best_big = masked_max(group_mine, group_ids, group_mine, group_ids, local_pos, local_pos)
    for distance in range(1, blocks // 2 + 1):
        others, other_ids = passed_along((group_mine, group_ids), "blk", distance)
        scores = score_block(group_mine, others)
        allowed = (group_ids[:, None] == other_ids[None, :]) & (group_ids[:, None] >= 0)
        masked = jnp.where(allowed, scores, -1.0)
        best_big = jnp.maximum(best_big, jnp.max(masked, axis=1))
        column_best = jnp.max(masked, axis=0)
        returned = passed_along(column_best, "blk", -distance)
        best_big = jnp.maximum(best_big, returned)
    big_return = lax.all_to_all(
        best_big.reshape(shards, cap_big), "docs", split_axis=0, concat_axis=0, tiled=True
    ).reshape(-1)
    small_return = lax.all_to_all(
        best_small.reshape(shards * blocks, cap_small),
        ("docs", "blk"),
        split_axis=0,
        concat_axis=0,
        tiled=True,
    ).reshape(-1)
    from_big = big_return[jnp.minimum(big_slot, shards * cap_big - 1)]
    from_small = small_return[jnp.minimum(small_slot, shards * blocks * cap_small - 1)]
    return jnp.where(is_big, from_big, from_small)


def solution(mesh):
    in_specs = (P(("slab", "docs", "blk"), None), P(), P(("slab", "docs", "blk")))
    out_specs = P(("slab", "docs", "blk"))
    return jax.shard_map(body, mesh=mesh, in_specs=in_specs, out_specs=out_specs, check_vma=False)
```

profile of v0, /device:TPU:0, one launch (start us, length us, event | category | flops | bytes accessed | tf_op | source)
XLA Modules:
  0.0 124.8 jit_solution(11843956203275217251)
XLA Ops:
  0.0 0.8 add_select_fusion.4
  0.8 1.2 reduce-window.6
  2.0 0.2 slice_reduce_fusion
  2.2 0.1 broadcast_add_fusion
  2.4 0.7 compare_select_fusion
  3.1 2.6 %scatter_custom_fusion = s32[256]{0:T(256)S(1)} fusion(s32[512]{0:T(512)S(1)} %get-tuple-element.14, s32[512]{0:T(512)} %param.5, s32[]{:T(128)} %constant.21.clone.1), kind=kCustom, calls=%fused_computation.65 | custom fusion | bytes 1536 | tf_op jit(solution)/shard_map/scatter | solution.py:65
  5.7 0.7 all_to_all.30
  6.4 4.2 %all-to-all-start = ((s32[4,1,64]{2,1,0:T(1,128)}), s32[4,1,64]{2,1,0:T(1,128)S(1)}, u32[]{:S(2)}, u32[]{:S(2)}) async-start(s32[4,1,64]{2,1,0:T(1,128)} %all_to_all.30), calls=%async_computation | async-start | bytes 4096 | tf_op jit(solution)/shard_map/all_to_all | solution.py:80
  10.6 2.0 %multiply_reduce_fusion = (f32[512]{0:T(512)S(1)}, f32[512,768]{1,0:T(8,128)S(1)}) fusion(bf16[512,768]{1,0:T(8,128)(2,1)} %param.3, bf16[768,768]{1,0:T(8,128)(2,1)S(1)} %copy-done), kind=kOutput, calls=%fused_computation.9 | convolution fusion | flops 604765696 | bytes 3540992 | tf_op jit(solution)/shard_map/dot_general | solution.py:39
  12.6 2.6 %scatter_custom_fusion.2 = s32[768]{0:T(1024)S(1)} fusion(s32[512]{0:T(512)S(1)} %get-tuple-element.16, s32[512]{0:T(512)} %param.5, s32[]{:T(128)} %constant.21.clone.1), kind=kCustom, calls=%fused_computation.55 | custom fusion | bytes 3584 | tf_op jit(solution)/shard_map/scatter | solution.py:76
  15.2 0.7 all_to_all.35
  15.9 6.9 %all-to-all-start.3 = ((s32[16,1,48]{2,1,0:T(1,128)}), s32[16,1,48]{2,1,0:T(1,128)S(1)}, u32[]{:S(2)}, u32[]{:S(2)}) async-start(s32[16,1,48]{2,1,0:T(1,128)} %all_to_all.35), calls=%async_computation.3 | async-start | bytes 16384 | tf_op jit(solution)/shard_map/all_to_all | solution.py:93
  22.8 3.4 %scatter_custom_fusion.1 = bf16[256,768]{1,0:T(8,128)(2,1)} fusion(s32[512]{0:T(512)S(1)} %get-tuple-element.14, bf16[]{:T(256)} %constant.57.clone.1, f32[512,768]{1,0:T(8,128)S(1)} %get-tuple-element.18, f32[512]{0:T(512)S(1)} %add_sqrt_fusion), kind=kCustom, calls=%fused_computation.29 | custom fusion | flops 786432 | bytes 1968130 | tf_op jit(solution)/shard_map/scatter | solution.py:59
  26.2 3.0 %all-to-all-done.3 = s32[16,1,48]{2,1,0:T(1,128)S(1)} async-done(((s32[16,1,48]{2,1,0:T(1,128)}), s32[16,1,48]{2,1,0:T(1,128)S(1)}, u32[]{:S(2)}, u32[]{:S(2)}) %all-to-all-start.3) | async-done | bytes 3104 | tf_op jit(solution)/shard_map/all_to_all | solution.py:93
  29.2 3.5 %all-to-all-start.1 = ((bf16[4,64,768]{2,1,0:T(8,128)(2,1)}), bf16[4,64,768]{2,1,0:T(8,128)(2,1)S(1)}, u32[]{:S(2)}, u32[]{:S(2)}) async-start(bf16[4,64,768]{2,1,0:T(8,128)(2,1)} %bitcast.2), calls=%async_computation.1 | async-start | bytes 786432 | tf_op jit(solution)/shard_map/all_to_all | solution.py:79
  32.6 3.6 %scatter_custom_fusion.3 = bf16[768,768]{1,0:T(8,128)(2,1)} fusion(s32[512]{0:T(512)S(1)} %get-tuple-element.16, bf16[]{:T(256)} %constant.57.clone.1, f32[512,768]{1,0:T(8,128)S(1)} %get-tuple-element.18, f32[512]{0:T(512)S(1)} %add_sqrt_fusion), kind=kCustom, calls=%fused_computation.18 | custom fusion | flops 786432 | bytes 2754562 | tf_op jit(solution)/shard_map/scatter | solution.py:71
  36.3 3.7 %all-to-all-done.1 = bf16[4,64,768]{2,1,0:T(8,128)(2,1)S(1)} async-done(((bf16[4,64,768]{2,1,0:T(8,128)(2,1)}), bf16[4,64,768]{2,1,0:T(8,128)(2,1)S(1)}, u32[]{:S(2)}, u32[]{:S(2)}) %all-to-all-start.1) | async-done | bytes 393248 | tf_op jit(solution)/shard_map/all_to_all | solution.py:79
  40.0 3.7 %all-to-all-start.4 = ((bf16[16,48,768]{2,1,0:T(8,128)(2,1)}), bf16[16,48,768]{2,1,0:T(8,128)(2,1)S(1)}, u32[]{:S(2)}, u32[]{:S(2)}) async-start(bf16[16,48,768]{2,1,0:T(8,128)(2,1)} %bitcast.24), calls=%async_computation.4 | async-start | bytes 2359296 | tf_op jit(solution)/shard_map/all_to_all | solution.py:86
  43.8 0.5 broadcast.121
  44.3 0.7 reduce.14
  44.9 0.1 eq.96
  45.0 1.8 %collective-permute-start = (s32[256]{0:T(256)S(1)}, s32[256]{0:T(256)S(1)}, u32[]{:S(2)}, u32[]{:S(2)}) collective-permute-start(s32[256]{0:T(256)S(1)} %eq.96), channel_id=1, source_target_pairs={{0,1},{1,2},{2,3},{3,0},{4,5},{5,6},{6,7},{7,4},{8,9},{9,10},{10,1... | collective-permute-start | bytes 3080 | tf_op jit(solution)/shard_map/ppermute | solution.py:11
  46.8 2.4 %collective-permute-start.3 = (s32[256]{0:T(256)S(1)}, s32[256]{0:T(256)S(1)}, u32[]{:S(2)}, u32[]{:S(2)}) collective-permute-start(s32[256]{0:T(256)S(1)} %eq.96), channel_id=1, source_target_pairs={{0,2},{1,3},{2,0},{3,1},{4,6},{5,7},{6,4},{7,5},{8,10},{9,11},{10,... | collective-permute-start | bytes 3080 | tf_op jit(solution)/shard_map/ppermute | solution.py:11
  49.2 0.7 reduce.16
  50.0 0.6 collective-permute-start.4
  50.6 1.5 %collective-permute-start.1 = (bf16[256,768]{1,0:T(8,128)(2,1)S(1)}, bf16[256,768]{1,0:T(8,128)(2,1)S(1)}, u32[]{:S(2)}, u32[]{:S(2)}) collective-permute-start(bf16[256,768]{1,0:T(8,128)(2,1)S(1)} %bitcast.26), channel_id=1, source_target_pairs={{0,1},{1,2},{2,3},{3,0},{4,5},{5,6},{6,7},{7,4},{8,9},{9,10},{10,1... | collective-permute-start | bytes 1179656 | tf_op jit(solution)/shard_map/ppermute | solution.py:11
  52.1 46.2 %collective-permute-done.4 = bf16[256,768]{1,0:T(8,128)(2,1)S(1)} collective-permute-done((bf16[256,768]{1,0:T(8,128)(2,1)S(1)}, bf16[256,768]{1,0:T(8,128)(2,1)S(1)}, u32[]{:S(2)}, u32[]{:S(2)}) %collective-permute-start.4) | collective-permute-done | bytes 393248 | tf_op jit(solution)/shard_map/ppermute | solution.py:11
  98.3 0.3 fusion.24
  98.6 0.4 fusion.10
  99.1 0.1 collective-permute-start.5
  99.2 0.5 collective-permute-start.2
  99.7 0.3 fusion.2
  100.0 3.6 %collective-permute-done.5 = f32[256]{0:T(256)S(1)} collective-permute-done((f32[256]{0:T(256)S(1)}, f32[256]{0:T(256)S(1)}, u32[]{:S(2)}, u32[]{:S(2)}) %collective-permute-start.5) | collective-permute-done | bytes 1056 | tf_op jit(solution)/shard_map/ppermute | solution.py:11
  103.6 0.7 all_to_all.33
  104.3 3.2 %all-to-all-start.2 = ((f32[4,1,64]{2,1,0:T(1,128)}), f32[4,1,64]{2,1,0:T(1,128)S(1)}, u32[]{:S(2)}, u32[]{:S(2)}) async-start(f32[4,1,64]{2,1,0:T(1,128)} %all_to_all.33), calls=%async_computation.2 | async-start | bytes 4096 | tf_op jit(solution)/shard_map/all_to_all | solution.py:131
  107.6 0.6 fusion.1
  108.2 1.1 select_reduce_fusion
  109.3 0.7 all_to_all.38
  110.0 1.2 all-to-all-done.2
  111.2 3.6 %all-to-all-start.5 = ((f32[16,1,48]{2,1,0:T(1,128)}), f32[16,1,48]{2,1,0:T(1,128)S(1)}, u32[]{:S(2)}, u32[]{:S(2)}) async-start(f32[16,1,48]{2,1,0:T(1,128)} %all_to_all.38), calls=%async_computation.5 | async-start | bytes 16384 | tf_op jit(solution)/shard_map/all_to_all | solution.py:134
  114.8 0.5 broadcast.122
  115.3 0.7 reduce.15
  116.0 0.1 reshape.91
  116.1 3.5 %gather_fusion = f32[512]{0:T(512)S(1)} fusion(f32[256]{0:T(256)S(1)} %reshape.91, s32[1024]{0:T(1024)S(1)} %get-tuple-element.20), kind=kCustom, calls=%fused_computation | custom fusion | bytes 6144 | tf_op jit(solution)/shard_map/gather | solution.py:141
  119.6 1.6 %all-to-all-done.5 = f32[16,1,48]{2,1,0:T(1,128)S(1)} async-done(((f32[16,1,48]{2,1,0:T(1,128)}), f32[16,1,48]{2,1,0:T(1,128)S(1)}, u32[]{:S(2)}, u32[]{:S(2)}) %all-to-all-start.5) | async-done | bytes 3104 | tf_op jit(solution)/shard_map/all_to_all | solution.py:134
  121.2 0.7 reduce.17
  122.0 2.3 %gather_fusion.1 = f32[512]{0:T(512)S(1)} fusion(f32[768]{0:T(1024)S(1)} %reshape.95, s32[1024]{0:T(1024)S(1)} %get-tuple-element.19), kind=kCustom, calls=%fused_computation.1 | custom fusion | bytes 6144 | tf_op jit(solution)/shard_map/gather | solution.py:142
  124.2 0.6 select_n.73
  (33 shorter events, 0.4 us)
Async XLA Ops:
  0.0 10.6 %copy-start = (bf16[768,768]{1,0:T(8,128)(2,1)S(1)}, bf16[768,768]{1,0:T(8,128)(2,1)}, u32[]{:S(2)}) copy-start(bf16[768,768]{1,0:T(8,128)(2,1)} %param.4) | copy-start | bytes 3538948
  6.4 9.5 %all-to-all-start = ((s32[4,1,64]{2,1,0:T(1,128)}), s32[4,1,64]{2,1,0:T(1,128)S(1)}, u32[]{:S(2)}, u32[]{:S(2)}) async-start(s32[4,1,64]{2,1,0:T(1,128)} %all_to_all.30), calls=%async_computation | async-start | bytes 4096 | tf_op jit(solution)/shard_map/all_to_all | solution.py:80
  15.9 13.3 %all-to-all-start.3 = ((s32[16,1,48]{2,1,0:T(1,128)}), s32[16,1,48]{2,1,0:T(1,128)S(1)}, u32[]{:S(2)}, u32[]{:S(2)}) async-start(s32[16,1,48]{2,1,0:T(1,128)} %all_to_all.35), calls=%async_computation.3 | async-start | bytes 16384 | tf_op jit(solution)/shard_map/all_to_all | solution.py:93
  29.2 10.8 %all-to-all-start.1 = ((bf16[4,64,768]{2,1,0:T(8,128)(2,1)}), bf16[4,64,768]{2,1,0:T(8,128)(2,1)S(1)}, u32[]{:S(2)}, u32[]{:S(2)}) async-start(bf16[4,64,768]{2,1,0:T(8,128)(2,1)} %bitcast.2), calls=%async_computation.1 | async-start | bytes 786432 | tf_op jit(solution)/shard_map/all_to_all | solution.py:79
  40.0 64.3 %all-to-all-start.4 = ((bf16[16,48,768]{2,1,0:T(8,128)(2,1)}), bf16[16,48,768]{2,1,0:T(8,128)(2,1)S(1)}, u32[]{:S(2)}, u32[]{:S(2)}) async-start(bf16[16,48,768]{2,1,0:T(8,128)(2,1)} %bitcast.24), calls=%async_computation.4 | async-start | bytes 2359296 | tf_op jit(solution)/shard_map/all_to_all | solution.py:86
  43.8 55.3 %copy-start.1 = (s32[768]{0:T(1024)}, s32[768]{0:T(1024)S(1)}, u32[]{:S(2)}) copy-start(s32[768]{0:T(1024)S(1)} %iota.24) | copy-start | bytes 9220
  45.0 53.6 %collective-permute-start = (s32[256]{0:T(256)S(1)}, s32[256]{0:T(256)S(1)}, u32[]{:S(2)}, u32[]{:S(2)}) collective-permute-start(s32[256]{0:T(256)S(1)} %eq.96), channel_id=1, source_target_pairs={{0,1},{1,2},{2,3},{3,0},{4,5},{5,6},{6,7},{7,4},{8,9},{9,10},{10,1... | collective-permute-start | bytes 3080 | tf_op jit(solution)/shard_map/ppermute | solution.py:11
  46.8 51.8 %collective-permute-start.3 = (s32[256]{0:T(256)S(1)}, s32[256]{0:T(256)S(1)}, u32[]{:S(2)}, u32[]{:S(2)}) collective-permute-start(s32[256]{0:T(256)S(1)} %eq.96), channel_id=1, source_target_pairs={{0,2},{1,3},{2,0},{3,1},{4,6},{5,7},{6,4},{7,5},{8,10},{9,11},{10,... | collective-permute-start | bytes 3080 | tf_op jit(solution)/shard_map/ppermute | solution.py:11
  50.0 48.3 %collective-permute-start.4 = (bf16[256,768]{1,0:T(8,128)(2,1)S(1)}, bf16[256,768]{1,0:T(8,128)(2,1)S(1)}, u32[]{:S(2)}, u32[]{:S(2)}) collective-permute-start(bf16[256,768]{1,0:T(8,128)(2,1)S(1)} %bitcast.25), channel_id=1, source_target_pairs={{0,2},{1,3},{2,0},{3,1},{4,6},{5,7},{6,4},{7,5},{8,10},{9,11},{10,... | collective-permute-start | bytes 1179656 | tf_op jit(solution)/shard_map/ppermute | solution.py:11
  50.6 48.0 %collective-permute-start.1 = (bf16[256,768]{1,0:T(8,128)(2,1)S(1)}, bf16[256,768]{1,0:T(8,128)(2,1)S(1)}, u32[]{:S(2)}, u32[]{:S(2)}) collective-permute-start(bf16[256,768]{1,0:T(8,128)(2,1)S(1)} %bitcast.26), channel_id=1, source_target_pairs={{0,1},{1,2},{2,3},{3,0},{4,5},{5,6},{6,7},{7,4},{8,9},{9,10},{10,1... | collective-permute-start | bytes 1179656 | tf_op jit(solution)/shard_map/ppermute | solution.py:11
  99.1 4.5 %collective-permute-start.5 = (f32[256]{0:T(256)S(1)}, f32[256]{0:T(256)S(1)}, u32[]{:S(2)}, u32[]{:S(2)}) collective-permute-start(f32[256]{0:T(256)S(1)} %get-tuple-element.9), channel_id=1, source_target_pairs={{0,2},{1,3},{2,0},{3,1},{4,6},{5,7},{6,4},{7,5},{8,10},{9,11},{10,... | collective-permute-start | bytes 3080 | tf_op jit(solution)/shard_map/ppermute | solution.py:11
  99.2 4.4 %collective-permute-start.2 = (f32[256]{0:T(256)S(1)}, f32[256]{0:T(256)S(1)}, u32[]{:S(2)}, u32[]{:S(2)}) collective-permute-start(f32[256]{0:T(256)S(1)} %get-tuple-element.6), channel_id=1, source_target_pairs={{0,3},{1,0},{2,1},{3,2},{4,7},{5,4},{6,5},{7,6},{8,11},{9,8},{10,9... | collective-permute-start | bytes 3080 | tf_op jit(solution)/shard_map/ppermute | solution.py:11
  104.3 6.9 %all-to-all-start.2 = ((f32[4,1,64]{2,1,0:T(1,128)}), f32[4,1,64]{2,1,0:T(1,128)S(1)}, u32[]{:S(2)}, u32[]{:S(2)}) async-start(f32[4,1,64]{2,1,0:T(1,128)} %all_to_all.33), calls=%async_computation.2 | async-start | bytes 4096 | tf_op jit(solution)/shard_map/all_to_all | solution.py:131
  107.5 0.7 slice-start
  111.2 10.0 %all-to-all-start.5 = ((f32[16,1,48]{2,1,0:T(1,128)}), f32[16,1,48]{2,1,0:T(1,128)S(1)}, u32[]{:S(2)}, u32[]{:S(2)}) async-start(f32[16,1,48]{2,1,0:T(1,128)} %all_to_all.38), calls=%async_computation.5 | async-start | bytes 16384 | tf_op jit(solution)/shard_map/all_to_all | solution.py:134
where the time goes:
time: 125 us
  waiting for transfers between devices  59.4 us (48%)
  starting transfers between devices  31.9 us (26%)
  local copies, waits for them, and re-layouts  15.3 us (12%)
  other arithmetic  13.2 us (11%)
  matrix products  4.74 us (4%)
    ppermute x6, waiting for transfers between devices, passed_along(): lax.ppermute(shard, axis, [(i, (i + by) % count) for i in range(count)])  49.9 us
    all_to_all x1, starting transfers between devices, body(): lax.all_to_all(small_ids.reshape(shards * blocks, cap_small), ('docs', 'b...  6.88 us
    ppermute x6, starting transfers between devices, passed_along(): lax.ppermute(shard, axis, [(i, (i + by) % count) for i in range(count)])  6.82 us
    all_to_all x1, starting transfers between devices, body(): lax.all_to_all(big_ids, 'docs', split_axis=0, concat_axis=0, tiled=True)  4.24 us
    all_to_all x1, waiting for transfers between devices, body(): lax.all_to_all(send_big, 'docs', split_axis=0, concat_axis=0, tiled=True)  3.73 us
    all_to_all x1, starting transfers between devices, body(): lax.all_to_all(send_small.reshape(shards * blocks, cap_small, feature), (...  3.7 us
    scatter x1, other arithmetic, body(): send_small = jnp.zeros((shards * blocks * cap_small, feature), jnp.bfloat...  3.64 us
    all_to_all x1, starting transfers between devices, body(): lax.all_to_all(best_small.reshape(shards * blocks, cap_small), ('docs', '...  3.58 us
  transfers between devices with their start and end apart: 12, of which 6 were waited for; matrix products, arithmetic and copies ran while one was open for 17% of the time, Pallas kernels for 0%

commit v1 on v0

v1 whole, which is shorter than its diff:
```python
import functools

import jax
import jax.numpy as jnp
from jax import lax
from jax.experimental import pallas as pl
from jax.experimental.pallas import tpu as pltpu
from jax.sharding import PartitionSpec as P

MESH = pl.DeviceIdType.MESH
BIG_OWN = 4
LANES = 128
F32 = jnp.float32
BF16 = jnp.bfloat16


def up(value, step):
    return -(-value // step) * step


def iota(shape, dim):
    return lax.broadcasted_iota(jnp.int32, shape, dim)


def nt(a, b):
    return lax.dot_general(a, b, (((1,), (1,)), ((), ())), preferred_element_type=F32)


def exact_dot(a, b):
    return jnp.dot(a, b, preferred_element_type=F32, precision=lax.Precision.HIGHEST)


def kernel(
    dims, pooled_hbm, weight_hbm, cluster_ref, out_ref,
    pooled, weight, embedded, small_send, small_recv, big_send, big_all,
    ids_send, ids_recv, big_marks, back_send, back_recv,
    in_sem, ids_ss, ids_rs, small_ss, small_rs, one_ss, one_rs, two_ss, two_rs,
    sback_ss, sback_rs, bback_ss, bback_rs,
):
    shards, blocks, cs, cb = dims
    n = shards * blocks
    rows = pooled.shape[0]
    nb = back_recv.shape[0]
    limit = BIG_OWN * shards
    me_d, me_b = lax.axis_index("docs"), lax.axis_index("blk")
    me = me_b * shards + me_d
    group = blocks * cb
    offsets = [blocks // 2] + [j for j in range(blocks) if j not in (0, blocks // 2)] + [0]
    peers = []
    for boff in offsets:
        for doff in range(shards - 1, -1, -1):
            if (boff, doff) != (0, 0):
                b, d = lax.rem(me_b + boff, blocks), lax.rem(me_d + doff, shards)
                peers.append((boff, d, b, b * shards + d))
    line = [lax.rem(me_b + boff, blocks) for boff in offsets if boff]
    cross = [lax.rem(me_d + doff, shards) for doff in range(1, shards)]

    load_rows = pltpu.make_async_copy(pooled_hbm, pooled, in_sem.at[0])
    load_weight = pltpu.make_async_copy(weight_hbm, weight, in_sem.at[1])
    load_rows.start()
    load_weight.start()
    barrier = pltpu.get_barrier_semaphore()
    for _, d, b, q in peers:
        pl.semaphore_signal(barrier, inc=1, device_id={"docs": d, "blk": b}, device_id_type=MESH)

    def copy(src, dst, ssem, rsem, d, b):
        return pltpu.make_async_remote_copy(
            src_ref=src, dst_ref=dst, send_sem=ssem, recv_sem=rsem,
            device_id={"docs": d, "blk": b}, device_id_type=MESH,
        )

    def ids_copy(to, slot, d, b):
        return copy(ids_send.at[to], ids_recv.at[slot], ids_ss.at[to], ids_rs.at[slot], d, b)

    def rows_at(ref, index, size):
        return ref.at[pl.ds(pl.multiple_of(index * size, 16), size)]

    def small_copy(to, slot, d, b):
        return copy(rows_at(small_send, to, cs), rows_at(small_recv, slot, cs), small_ss.at[to], small_rs.at[slot], d, b)

    def one_copy(to, slot, d, b):
        return copy(rows_at(big_send, to, cb), rows_at(big_all, me_d * blocks + slot, cb), one_ss.at[to], one_rs.at[slot], d, b)

    def two_copy(to, slot, d, b):
        return copy(rows_at(big_all, me_d, group), rows_at(big_all, slot, group), two_ss.at[to], two_rs.at[slot], d, b)

    def sback_copy(to, slot, d, b):
        return copy(back_send.at[to], back_recv.at[slot], sback_ss.at[to], sback_rs.at[slot], d, b)

    def bback_copy(to, slot, d, b):
        return copy(back_send.at[n + to], back_recv.at[n + slot], bback_ss.at[to], bback_rs.at[slot], d, b)

    cluster = cluster_ref[...]
    is_big = cluster < limit
    lane_rest = cluster - limit
    bucket = jnp.where(is_big, n + lax.rem(cluster, blocks), lax.rem(jnp.maximum(lane_rest, 0), n))
    local_id = jnp.where(is_big, cluster // blocks, jnp.maximum(lane_rest, 0) // n) + 1
    onehot = iota((nb, rows), 0) == bucket
    before = jnp.dot(
        onehot.astype(BF16), (iota((rows, rows), 0) < iota((rows, rows), 1)).astype(BF16),
        preferred_element_type=F32,
    )
    rank = jnp.sum(jnp.where(onehot, before, 0.0), axis=0, keepdims=True).astype(jnp.int32)
    at_rank = iota((LANES, rows), 0) == rank
    ids = nt(jnp.where(onehot, local_id.astype(F32), 0.0).astype(BF16), at_rank.astype(BF16))
    first = iota((8, LANES), 0) == 0
    for q in range(n):
        g = n + q // shards
        ids_send[q] = jnp.where(
            first, jnp.broadcast_to(ids[q : q + 1], (8, LANES)), jnp.broadcast_to(ids[g : g + 1], (8, LANES))
        )
    ids_recv[me] = ids_send[me]
    for q in range(n + blocks, nb):
        back_recv[q] = jnp.zeros((8, LANES), F32)

    load_rows.wait()
    load_weight.wait()
    projected = jnp.dot(pooled[...], weight[...], preferred_element_type=F32)
    norm = jnp.sqrt(jnp.sum(projected * projected, axis=1, keepdims=True) + 1e-06)
    embedded[...] = (projected / norm).astype(BF16)
    big_slot = jnp.where(is_big, (bucket - n) * cb + rank, -1)
    pick = (iota((group, rows), 0) == big_slot).astype(BF16)
    big_send[...] = jnp.dot(pick, embedded[...], preferred_element_type=F32).astype(BF16)

    pl.semaphore_wait(barrier, n - 1)
    for b in line:
        one_copy(b, me_b, me_d, b).start()
    for _, d, b, q in peers:
        ids_copy(q, me, d, b).start()
    own = pl.ds(pl.multiple_of((me_d * blocks + me_b) * cb, 16), cb)
    big_all[own, :] = big_send[pl.ds(pl.multiple_of(me_b * cb, 16), cb), :]

    span = shards * cs
    small_slot = jnp.where(is_big, -1, bucket * cs + rank)
    for boff in offsets:
        b = lax.rem(me_b + boff, blocks)
        pick = (iota((span, rows), 0) + b * span == small_slot).astype(BF16)
        small_send[pl.ds(pl.multiple_of(b * span, 16), span), :] = jnp.dot(
            pick, embedded[...], preferred_element_type=F32
        ).astype(BF16)
        for at, d, b2, q in peers:
            if at == boff:
                small_copy(q, me, d, b2).start()
    own = pl.ds(pl.multiple_of(me * cs, 16), cs)
    small_recv[own, :] = small_send[own, :]

    for b in line:
        one_copy(b, b, me_d, b).wait_recv()
    for d in cross:
        two_copy(d, me_d, d, me_b).start()

    for _, d, b, q in peers:
        ids_copy(q, q, d, b).wait_recv()
    total = n * cs
    low = iota((total, n), 1) * cs
    at = iota((total, n), 0)
    inside = (at >= low) & (at < low + cs)
    base = jnp.sum(jnp.where(inside, low, 0).astype(F32), axis=1, keepdims=True).astype(jnp.int32)
    small_lane = iota((total, LANES), 1) == iota((total, LANES), 0) - base
    marks = jnp.dot(inside.astype(BF16), ids_recv[:, 0, :].astype(BF16), preferred_element_type=F32)
    marks = jnp.where(small_lane, marks, 0.0)
    small_col = jnp.sum(marks, axis=1, keepdims=True)
    small_row = nt(jnp.ones((8, LANES), BF16), marks.astype(BF16))[0:1]

    big_total = n * cb
    source = iota((big_total, n), 1)
    low = (lax.rem(source, shards) * blocks + source // shards) * cb
    at = iota((big_total, n), 0)
    inside = (at >= low) & (at < low + cb)
    base = jnp.sum(jnp.where(inside, low, 0).astype(F32), axis=1, keepdims=True).astype(jnp.int32)
    marks = jnp.dot(inside.astype(BF16), ids_recv[:, 1, :].astype(BF16), preferred_element_type=F32)
    big_marks[...] = jnp.where(iota((big_total, LANES), 1) == iota((big_total, LANES), 0) - base, marks, 0.0)

    mine = pl.ds(pl.multiple_of(me_d * group, 16), group)
    my_row = nt(jnp.ones((8, LANES), BF16), big_marks[mine, :].astype(BF16))[0:1]
    best = jnp.full((1, group), -1.0, F32)
    for d in [me_d] + cross:
        if d is not me_d:
            two_copy(d, d, d, me_b).wait_recv()
        theirs = pl.ds(pl.multiple_of(d * group, 16), group)
        scores = nt(big_all[theirs, :], big_all[mine, :])
        allowed = jnp.sum(big_marks[theirs, :], axis=1, keepdims=True) == my_row
        if d is me_d:
            allowed = allowed & (iota((group, group), 0) != iota((group, group), 1))
        best = jnp.maximum(best, jnp.max(jnp.where(allowed, scores, -1.0), axis=0, keepdims=True))
    low = iota((blocks, group), 0) * cb
    at = iota((blocks, group), 1)
    spread = jnp.where((at >= low) & (at < low + cb), best, 0.0)
    place = lax.rem(iota((group, LANES), 0), cb) == iota((group, LANES), 1)
    back = exact_dot(spread, place.astype(F32))
    for b in range(blocks):
        back_send[n + b] = jnp.broadcast_to(back[b : b + 1], (8, LANES))
    for b in line:
        bback_copy(b, me_b, me_d, b).start()
    back_recv[n + me_b] = back_send[n + me_b]

    for _, d, b, q in peers:
        small_copy(q, q, d, b).wait_recv()
    width = next(w for w in (256, 128, total) if total % w == 0)
    parts = []
    for start in range(0, total, width):
        scores = nt(small_recv[...], small_recv[start : start + width, :])
        allowed = (small_col == small_row[:, start : start + width]) & (
            iota((total, width), 0) != iota((total, width), 1) + start
        )
        parts.append(jnp.max(jnp.where(allowed, scores, -1.0), axis=0, keepdims=True))
    best = jnp.concatenate(parts, axis=1) if len(parts) > 1 else parts[0]
    low = iota((n, total), 0) * cs
    at = iota((n, total), 1)
    spread = jnp.where((at >= low) & (at < low + cs), best, 0.0)
    back = exact_dot(spread, small_lane.astype(F32))
    for q in range(n):
        back_send[q] = jnp.broadcast_to(back[q : q + 1], (8, LANES))
    for _, d, b, q in peers:
        sback_copy(q, me, d, b).start()
    back_recv[me] = back_send[me]

    for b in line:
        bback_copy(b, b, me_d, b).wait_recv()
    for _, d, b, q in peers:
        sback_copy(q, q, d, b).wait_recv()
    result = exact_dot(back_recv[:, 0, :], at_rank.astype(F32))
    out_ref[...] = jnp.sum(jnp.where(onehot, result, 0.0), axis=0, keepdims=True)

    for b in line:
        one_copy(b, me_b, me_d, b).wait_send()
        bback_copy(b, me_b, me_d, b).wait_send()
    for d in cross:
        two_copy(d, me_d, d, me_b).wait_send()
    for _, d, b, q in peers:
        ids_copy(q, me, d, b).wait_send()
        small_copy(q, me, d, b).wait_send()
        sback_copy(q, me, d, b).wait_send()


def solution(mesh):
    shards, blocks = mesh.shape["docs"], mesh.shape["blk"]
    n = shards * blocks

    def body(pooled, proj_weight, cluster):
        rows, width = pooled.shape
        feature = proj_weight.shape[1]
        big_count = rows // 4
        cap_big = 2 * big_count // shards
        cap_small = 2 * (rows - big_count) // n
        cs = up(cap_small, 16)
        cb = up(cap_big * (shards // blocks), 16)
        nb = up(n + blocks, 16)
        dma = pltpu.SemaphoreType.DMA
        out = pl.pallas_call(
            functools.partial(kernel, (shards, blocks, cs, cb)),
            out_shape=jax.ShapeDtypeStruct((1, rows), F32),
            in_specs=[
                pl.BlockSpec(memory_space=pl.ANY),
                pl.BlockSpec(memory_space=pl.ANY),
                pl.BlockSpec(memory_space=pltpu.VMEM),
            ],
            out_specs=pl.BlockSpec(memory_space=pltpu.VMEM),
            scratch_shapes=[
                pltpu.VMEM((rows, width), BF16),
                pltpu.VMEM((width, feature), BF16),
                pltpu.VMEM((rows, feature), BF16),
                pltpu.VMEM((n * cs, feature), BF16),
                pltpu.VMEM((n * cs, feature), BF16),
                pltpu.VMEM((blocks * cb, feature), BF16),
                pltpu.VMEM((n * cb, feature), BF16),
                pltpu.VMEM((n, 8, LANES), F32),
                pltpu.VMEM((n, 8, LANES), F32),
                pltpu.VMEM((n * cb, LANES), F32),
                pltpu.VMEM((n + blocks, 8, LANES), F32),
                pltpu.VMEM((nb, 8, LANES), F32),
                dma((2,)), dma((n,)), dma((n,)), dma((n,)), dma((n,)), dma((blocks,)), dma((blocks,)),
                dma((shards,)), dma((shards,)), dma((n,)), dma((n,)), dma((blocks,)), dma((blocks,)),
            ],
            compiler_params=pltpu.CompilerParams(
                collective_id=0, has_side_effects=True, vmem_limit_bytes=60 * 1024 * 1024
            ),
        )(pooled, proj_weight, cluster.reshape(1, rows))
        return out.reshape(rows)

    in_specs = (P(("slab", "docs", "blk"), None), P(), P(("slab", "docs", "blk")))
    out_specs = P(("slab", "docs", "blk"))
    return jax.shard_map(body, mesh=mesh, in_specs=in_specs, out_specs=out_specs, check_vma=False)
```

time: 125 us -> 57.8 us (0.46)
  waiting for transfers between devices: 59.4 us -> 0 us
  Pallas kernels: 0 us -> 56.4 us
  starting transfers between devices: 31.9 us -> 0 us
  local copies, waits for them, and re-layouts: 15.3 us -> 1.26 us
  other arithmetic: 13.2 us -> 0 us
  matrix products: 4.74 us -> 0 us
    pallas_call x0 -> x1, Pallas kernels: none -> 56.4 us  [body(): pl.pallas_call(functools.partial(kernel, (shards, blocks, cs, cb)), out_s...]
    ppermute x6 -> x0, waiting for transfers between devices: 49.9 us -> none  [passed_along(): lax.ppermute(shard, axis, [(i, (i + by) % count) for i in range(count)])]
    all_to_all x6 -> x0, starting transfers between devices: 25.1 us -> none  [the longest x1 6.88 us: body(): lax.all_to_all(small_ids.reshape(shards * blocks, cap_small), ('docs', 'b...]
    all_to_all x6 -> x0, waiting for transfers between devices: 9.56 us -> none  [the longest x1 3.73 us: body(): lax.all_to_all(send_big, 'docs', split_axis=0, concat_axis=0, tiled=True)]
    scatter x2 -> x0, other arithmetic: 7.07 us -> none  [the longest x1 3.64 us: body(): send_small = jnp.zeros((shards * blocks * cap_small, feature), jnp.bfloat...]
    ppermute x6 -> x0, starting transfers between devices: 6.82 us -> none  [passed_along(): lax.ppermute(shard, axis, [(i, (i + by) % count) for i in range(count)])]
    gather x2 -> x0, local copies, waits for them, and re-layouts: 5.78 us -> none  [the longest x1 3.5 us: body(): from_big = big_return[jnp.minimum(big_slot, shards * cap_big - 1)]]
    scatter x2 -> x0, local copies, waits for them, and re-layouts: 5.2 us -> none  [the longest x1 2.6 us: body(): small_ids = jnp.full((shards * blocks * cap_small,), -1, jnp.int32).at[sm...]
  transfers between devices with their start and end apart: 12 -> 0, of which waited for: 6 -> 0; matrix products, arithmetic and copies ran while one was open for 17% -> 0% of each run, Pallas kernels for 0% -> 0%
where the time goes in v1:
time: 57.8 us; the launch traced here: 57.7 us
  Pallas kernels  56.4 us (98%)
  local copies, waits for them, and re-layouts  1.26 us (2%)
    pallas_call x1, Pallas kernels, body(): pl.pallas_call(functools.partial(kernel, (shards, blocks, cs, cb)), out_s...  56.4 us
    unnamed x1, local copies, waits for them, and re-layouts  1.26 us

profile of v1, /device:TPU:0, one launch (start us, length us, event | category | flops | bytes accessed | tf_op | source)
XLA Modules:
  0.0 57.7 jit_solution(6261823064668622503)
XLA Ops:
  0.0 56.4 %shard_map.37 = f32[1,512]{1,0:T(1,128)} custom-call(bf16[512,768]{1,0:T(8,128)(2,1)} %pooled_hbm.1, bf16[768,768]{1,0:T(8,128)(2,1)} %weight_hbm.1, s32[1,512]{1,0:T(1,128)} %bitcast.3), custom_call_target="tpu_custom_call" | custom-call | tf_op jit(solution)/shard_map/pallas_call | solution.py:250
  56.4 1.3 %copy.5 = f32[512]{0:T(512)} copy(f32[512]{0:T(512)} %bitcast.2) | data formatting | bytes 4096

commit v2 on v1

v2 whole, which is shorter than its diff:
```python
import functools

import jax
import jax.numpy as jnp
from jax import lax
from jax.experimental import pallas as pl
from jax.experimental.pallas import tpu as pltpu
from jax.sharding import PartitionSpec as P

MESH = pl.DeviceIdType.MESH
BIG_OWN = 4
LANES = 128
F32 = jnp.float32
BF16 = jnp.bfloat16


def up(value, step):
    return -(-value // step) * step


def iota(shape, dim):
    return lax.broadcasted_iota(jnp.int32, shape, dim)


def nt(a, b):
    return lax.dot_general(a, b, (((1,), (1,)), ((), ())), preferred_element_type=F32)


def exact_dot(a, b):
    return jnp.dot(a, b, preferred_element_type=F32, precision=lax.Precision.HIGHEST)


def kernel(
    dims, pooled_hbm, weight_hbm, cluster_ref, out_ref,
    pooled, weight, embedded, small_send, relay, small_recv, big_send, big_all,
    ids_send, ids_recv, big_marks, back_send, back_recv,
    in_sem, ids_ss, ids_rs, side_ss, side_rs, small_ss, small_rs, one_ss, one_rs, two_ss, two_rs,
    sback_ss, sback_rs, bback_ss, bback_rs,
):
    shards, blocks, cs, cb = dims
    n = shards * blocks
    rows = pooled.shape[0]
    nb = back_recv.shape[0]
    limit = BIG_OWN * shards
    cores = 2 if shards % 2 == 0 else 1
    chips = shards // cores
    me_d, me_b = lax.axis_index("docs"), lax.axis_index("blk")
    me_x, me_c = me_d // cores, lax.rem(me_d, cores)
    group = blocks * cb
    far = [blocks // 2] + [j for j in range(1, blocks) if j != blocks // 2]

    def docs_at(r, sign=1):
        dx, dc = r // cores, r % cores
        return lax.rem(me_x + sign * dx + chips, chips) * cores + lax.rem(me_c + dc, cores)

    def blk_at(j, sign=1):
        return lax.rem(me_b + sign * j + blocks, blocks)

    peers = [(r * blocks + j, r, j) for j in far + [0] for r in range(shards - 1, -1, -1) if (r, j) != (0, 0)]

    load_rows = pltpu.make_async_copy(pooled_hbm, pooled, in_sem.at[0])
    load_weight = pltpu.make_async_copy(weight_hbm, weight, in_sem.at[1])
    load_rows.start()
    load_weight.start()
    barrier = pltpu.get_barrier_semaphore()
    for _, r, j in peers:
        pl.semaphore_signal(
            barrier, inc=1, device_id={"docs": docs_at(r), "blk": blk_at(j)}, device_id_type=MESH
        )

    def copy(src, dst, ssem, rsem, d, b):
        return pltpu.make_async_remote_copy(
            src_ref=src, dst_ref=dst, send_sem=ssem, recv_sem=rsem,
            device_id={"docs": d, "blk": b}, device_id_type=MESH,
        )

    def chunk(ref, index, size):
        return ref.at[pl.ds(index * size, size)]

    def ids_copy(q, r, j):
        return copy(ids_send.at[q], ids_recv.at[q], ids_ss.at[q], ids_rs.at[q], docs_at(r), blk_at(j))

    def side_copy(r, j):
        q = r * blocks + j
        into = small_recv if j == 0 else relay
        return copy(chunk(small_send, q, cs), chunk(into, q, cs), side_ss.at[q], side_rs.at[q], docs_at(r), me_b)

    def line_copy(r, j):
        q = r * blocks + j
        return copy(chunk(relay, q, cs), chunk(small_recv, q, cs), small_ss.at[q], small_rs.at[q], me_d, blk_at(j))

    def one_copy(j):
        return copy(chunk(big_send, j, cb), chunk(big_all, j, cb), one_ss.at[j], one_rs.at[j], me_d, blk_at(j))

    def two_copy(r):
        if r == 1 or r % cores == 0:
            return copy(chunk(big_all, 0, group), chunk(big_all, r, group), two_ss.at[r], two_rs.at[r], docs_at(r), me_b)
        return copy(
            chunk(big_all, r - 1, group), chunk(big_all, r, group), two_ss.at[r], two_rs.at[r], docs_at(1), me_b
        )

    def sback_copy(q, r, j):
        return copy(
            back_send.at[q], back_recv.at[q], sback_ss.at[q], sback_rs.at[q], docs_at(r, -1), blk_at(j, -1)
        )

    def bback_copy(j):
        return copy(back_send.at[n + j], back_recv.at[n + j], bback_ss.at[j], bback_rs.at[j], me_d, blk_at(j, -1))

    cluster = cluster_ref[...]
    is_big = cluster < limit
    rest = jnp.maximum(cluster - limit, 0)
    owner = lax.rem(rest, n)
    owner_b, owner_d = owner // shards, lax.rem(owner, shards)
    side = lax.rem(owner_d // cores - me_x + chips, chips) * cores + lax.rem(lax.rem(owner_d, cores) - me_c + cores, cores)
    small_bucket = side * blocks + lax.rem(owner_b - me_b + blocks, blocks)
    big_bucket = n + lax.rem(lax.rem(cluster, blocks) - me_b + blocks, blocks)
    bucket = jnp.where(is_big, big_bucket, small_bucket)
    local_id = jnp.where(is_big, cluster // blocks, rest // n) + 1
    onehot = iota((nb, rows), 0) == bucket
    before = jnp.dot(
        onehot.astype(BF16), (iota((rows, rows), 0) < iota((rows, rows), 1)).astype(BF16),
        preferred_element_type=F32,
    )
    rank = jnp.sum(jnp.where(onehot, before, 0.0), axis=0, keepdims=True).astype(jnp.int32)
    at_rank = iota((LANES, rows), 0) == rank
    ids = nt(jnp.where(onehot, local_id.astype(F32), 0.0).astype(BF16), at_rank.astype(BF16))
    first = iota((8, LANES), 0) == 0
    for q in range(n):
        g = n + q % blocks
        ids_send[q] = jnp.where(
            first, jnp.broadcast_to(ids[q : q + 1], (8, LANES)), jnp.broadcast_to(ids[g : g + 1], (8, LANES))
        )
    ids_recv[0] = ids_send[0]
    for q in range(n + blocks, nb):
        back_recv[q] = jnp.zeros((8, LANES), F32)

    load_rows.wait()
    load_weight.wait()
    projected = jnp.dot(pooled[...], weight[...], preferred_element_type=F32)
    norm = jnp.sqrt(jnp.sum(projected * projected, axis=1, keepdims=True) + 1e-06)
    embedded[...] = (projected / norm).astype(BF16)
    big_slot = jnp.where(is_big, (bucket - n) * cb + rank, -1)
    pick = (iota((group, rows), 0) == big_slot).astype(BF16)
    big_send[...] = jnp.dot(pick, embedded[...], preferred_element_type=F32).astype(BF16)

    pl.semaphore_wait(barrier, n - 1)
    for j in far:
        one_copy(j).start()
    for q, r, j in peers:
        ids_copy(q, r, j).start()
    big_all[0:cb, :] = big_send[0:cb, :]

    small_slot = jnp.where(is_big, -1, bucket * cs + rank)
    order = [r for r in range(cores, shards)] + [r for r in range(1, cores)] + [0]
    span = blocks * cs
    for r in order:
        pick = (iota((span, rows), 0) + r * span == small_slot).astype(BF16)
        picked = jnp.dot(pick, embedded[...], preferred_element_type=F32).astype(BF16)
        if r:
            small_send[r * span : (r + 1) * span, :] = picked
        else:
            relay[0:span, :] = picked
            small_recv[0:cs, :] = picked[0:cs]
        for j in far + [0]:
            if r:
                side_copy(r, j).start()
            elif j:
                line_copy(r, j).start()

    for r in range(1, shards):
        if r == cores:
            for j in far:
                one_copy(j).wait_recv()
            for r2 in range(1, shards):
                if r2 == 1 or r2 % cores == 0:
                    two_copy(r2).start()
        for j in far:
            side_copy(r, j).wait_recv()
            line_copy(r, j).start()

    for q, r, j in peers:
        ids_copy(q, r, j).wait_recv()
    total = n * cs
    low = iota((total, n), 1) * cs
    at = iota((total, n), 0)
    inside = (at >= low) & (at < low + cs)
    base = jnp.sum(jnp.where(inside, low, 0).astype(F32), axis=1, keepdims=True).astype(jnp.int32)
    small_lane = iota((total, LANES), 1) == iota((total, LANES), 0) - base
    marks = jnp.dot(inside.astype(BF16), ids_recv[:, 0, :].astype(BF16), preferred_element_type=F32)
    marks = jnp.where(small_lane, marks, 0.0)
    small_col = jnp.sum(marks, axis=1, keepdims=True)
    small_row = nt(jnp.ones((8, LANES), BF16), marks.astype(BF16))[0:1]

    big_total = n * cb
    low = iota((big_total, n), 1) * cb
    at = iota((big_total, n), 0)
    inside = (at >= low) & (at < low + cb)
    base = jnp.sum(jnp.where(inside, low, 0).astype(F32), axis=1, keepdims=True).astype(jnp.int32)
    marks = jnp.dot(inside.astype(BF16), ids_recv[:, 1, :].astype(BF16), preferred_element_type=F32)
    big_marks[...] = jnp.where(iota((big_total, LANES), 1) == iota((big_total, LANES), 0) - base, marks, 0.0)

    my_row = nt(jnp.ones((8, LANES), BF16), big_marks[0:group, :].astype(BF16))[0:1]
    best = jnp.full((1, group), -1.0, F32)
    for r in range(shards):
        if r:
            two_copy(r).wait_recv()
            if r % cores == 0 and cores > 1:
                two_copy(r + 1).start()
        theirs = pl.ds(r * group, group)
        scores = nt(big_all[theirs, :], big_all[0:group, :])
        allowed = jnp.sum(big_marks[theirs, :], axis=1, keepdims=True) == my_row
        if r == 0:
            allowed = allowed & (iota((group, group), 0) != iota((group, group), 1))
        best = jnp.maximum(best, jnp.max(jnp.where(allowed, scores, -1.0), axis=0, keepdims=True))
    low = iota((blocks, group), 0) * cb
    at = iota((blocks, group), 1)
    spread = jnp.where((at >= low) & (at < low + cb), best, 0.0)
    place = lax.rem(iota((group, LANES), 0), cb) == iota((group, LANES), 1)
    back = exact_dot(spread, place.astype(F32))
    for b in range(blocks):
        back_send[n + b] = jnp.broadcast_to(back[b : b + 1], (8, LANES))
    for j in far:
        bback_copy(j).start()
    back_recv[n] = back_send[n]

    for q, r, j in peers:
        (line_copy if j else side_copy)(r, j).wait_recv()
    width = next(w for w in (256, 128, total) if total % w == 0)
    parts = []
    for start in range(0, total, width):
        scores = nt(small_recv[...], small_recv[start : start + width, :])
        allowed = (small_col == small_row[:, start : start + width]) & (
            iota((total, width), 0) != iota((total, width), 1) + start
        )
        parts.append(jnp.max(jnp.where(allowed, scores, -1.0), axis=0, keepdims=True))
    best = jnp.concatenate(parts, axis=1) if len(parts) > 1 else parts[0]
    low = iota((n, total), 0) * cs
    at = iota((n, total), 1)
    spread = jnp.where((at >= low) & (at < low + cs), best, 0.0)
    back = exact_dot(spread, small_lane.astype(F32))
    for q in range(n):
        back_send[q] = jnp.broadcast_to(back[q : q + 1], (8, LANES))
    for q, r, j in peers:
        sback_copy(q, r, j).start()
    back_recv[0] = back_send[0]

    for j in far:
        bback_copy(j).wait_recv()
    for q, r, j in peers:
        sback_copy(q, r, j).wait_recv()
    result = exact_dot(back_recv[:, 0, :], at_rank.astype(F32))
    out_ref[...] = jnp.sum(jnp.where(onehot, result, 0.0), axis=0, keepdims=True)

    for j in far:
        one_copy(j).wait_send()
        bback_copy(j).wait_send()
    for r in range(1, shards):
        two_copy(r).wait_send()
    for q, r, j in peers:
        ids_copy(q, r, j).wait_send()
        sback_copy(q, r, j).wait_send()
        if r:
            side_copy(r, j).wait_send()
        if j:
            line_copy(r, j).wait_send()


def solution(mesh):
    shards, blocks = mesh.shape["docs"], mesh.shape["blk"]
    n = shards * blocks

    def body(pooled, proj_weight, cluster):
        rows, width = pooled.shape
        feature = proj_weight.shape[1]
        big_count = rows // 4
        cap_big = 2 * big_count // shards
        cap_small = 2 * (rows - big_count) // n
        cs = up(cap_small, 16)
        cb = up(cap_big * (shards // blocks), 16)
        nb = up(n + blocks, 16)
        dma = pltpu.SemaphoreType.DMA
        out = pl.pallas_call(
            functools.partial(kernel, (shards, blocks, cs, cb)),
            out_shape=jax.ShapeDtypeStruct((1, rows), F32),
            in_specs=[
                pl.BlockSpec(memory_space=pl.ANY),
                pl.BlockSpec(memory_space=pl.ANY),
                pl.BlockSpec(memory_space=pltpu.VMEM),
            ],
            out_specs=pl.BlockSpec(memory_space=pltpu.VMEM),
            scratch_shapes=[
                pltpu.VMEM((rows, width), BF16),
                pltpu.VMEM((width, feature), BF16),
                pltpu.VMEM((rows, feature), BF16),
                pltpu.VMEM((n * cs, feature), BF16),
                pltpu.VMEM((n * cs, feature), BF16),
                pltpu.VMEM((n * cs, feature), BF16),
                pltpu.VMEM((blocks * cb, feature), BF16),
                pltpu.VMEM((n * cb, feature), BF16),
                pltpu.VMEM((n, 8, LANES), F32),
                pltpu.VMEM((n, 8, LANES), F32),
                pltpu.VMEM((n * cb, LANES), F32),
                pltpu.VMEM((n + blocks, 8, LANES), F32),
                pltpu.VMEM((nb, 8, LANES), F32),
                dma((2,)), dma((n,)), dma((n,)), dma((n,)), dma((n,)), dma((n,)), dma((n,)), dma((blocks,)), dma((blocks,)),
                dma((shards,)), dma((shards,)), dma((n,)), dma((n,)), dma((blocks,)), dma((blocks,)),
            ],
            compiler_params=pltpu.CompilerParams(
                collective_id=0, has_side_effects=True, vmem_limit_bytes=60 * 1024 * 1024
            ),
        )(pooled, proj_weight, cluster.reshape(1, rows))
        return out.reshape(rows)

    in_specs = (P(("slab", "docs", "blk"), None), P(), P(("slab", "docs", "blk")))
    out_specs = P(("slab", "docs", "blk"))
    return jax.shard_map(body, mesh=mesh, in_specs=in_specs, out_specs=out_specs, check_vma=False)
```

time: 57.8 us -> 52.8 us (0.913)
  Pallas kernels: 56.4 us -> 51.4 us
    pallas_call x1, Pallas kernels: 56.4 us -> 51.4 us  [body(): pl.pallas_call(functools.partial(kernel, (shards, blocks, cs, cb)), out_s...]
where the time goes in v2:
time: 52.8 us; the launch traced here: 52.6 us
  Pallas kernels  51.4 us (97%)
  local copies, waits for them, and re-layouts  1.26 us (2%)
    pallas_call x1, Pallas kernels, body(): pl.pallas_call(functools.partial(kernel, (shards, blocks, cs, cb)), out_s...  51.4 us
    unnamed x1, local copies, waits for them, and re-layouts  1.26 us

profile of v2, /device:TPU:0, one launch (start us, length us, event | category | flops | bytes accessed | tf_op | source)
XLA Modules:
  0.0 52.6 jit_solution(2953281407729567883)
XLA Ops:
  0.0 51.4 %shard_map.37 = f32[1,512]{1,0:T(1,128)} custom-call(bf16[512,768]{1,0:T(8,128)(2,1)} %pooled_hbm.1, bf16[768,768]{1,0:T(8,128)(2,1)} %weight_hbm.1, s32[1,512]{1,0:T(1,128)} %bitcast.3), custom_call_target="tpu_custom_call" | custom-call | tf_op jit(solution)/shard_map/pallas_call | solution.py:283
  51.4 1.3 %copy.5 = f32[512]{0:T(512)} copy(f32[512]{0:T(512)} %bitcast.2) | data formatting | bytes 4096

commit v3 on v2

--- a/solution.py
+++ b/solution.py
@@ -27,7 +27,13 @@
 
 
 def exact_dot(a, b):
-    return jnp.dot(a, b, preferred_element_type=F32, precision=lax.Precision.HIGHEST)
+    high = a.astype(BF16)
+    rest = a - high.astype(F32)
+    middle = rest.astype(BF16)
+    low = (rest - middle.astype(F32)).astype(BF16)
+    three = jnp.dot(jnp.concatenate([high, middle, low], axis=0), b.astype(BF16), preferred_element_type=F32)
+    m = a.shape[0]
+    return three[:m] + three[m : 2 * m] + three[2 * m :]
 
 
 def kernel(
@@ -48,6 +54,7 @@
     me_x, me_c = me_d // cores, lax.rem(me_d, cores)
     group = blocks * cb
     far = [blocks // 2] + [j for j in range(1, blocks) if j != blocks // 2]
+    steps = far
 
     def docs_at(r, sign=1):
         dx, dc = r // cores, r % cores
@@ -82,7 +89,7 @@
 
     def side_copy(r, j):
         q = r * blocks + j
-        into = small_recv if j == 0 else relay
+        into = small_recv if isinstance(j, int) and j == 0 else relay
         return copy(chunk(small_send, q, cs), chunk(into, q, cs), side_ss.at[q], side_rs.at[q], docs_at(r), me_b)
 
     def line_copy(r, j):
@@ -125,15 +132,12 @@
     rank = jnp.sum(jnp.where(onehot, before, 0.0), axis=0, keepdims=True).astype(jnp.int32)
     at_rank = iota((LANES, rows), 0) == rank
     ids = nt(jnp.where(onehot, local_id.astype(F32), 0.0).astype(BF16), at_rank.astype(BF16))
-    first = iota((8, LANES), 0) == 0
     for q in range(n):
         g = n + q % blocks
-        ids_send[q] = jnp.where(
-            first, jnp.broadcast_to(ids[q : q + 1], (8, LANES)), jnp.broadcast_to(ids[g : g + 1], (8, LANES))
-        )
+        ids_send[q] = jnp.concatenate([ids[q : q + 1], ids[g : g + 1]], axis=1)
     ids_recv[0] = ids_send[0]
     for q in range(n + blocks, nb):
-        back_recv[q] = jnp.zeros((8, LANES), F32)
+        back_recv[q] = jnp.zeros((1, LANES), F32)
 
     load_rows.wait()
     load_weight.wait()
@@ -144,11 +148,6 @@
     pick = (iota((group, rows), 0) == big_slot).astype(BF16)
     big_send[...] = jnp.dot(pick, embedded[...], preferred_element_type=F32).astype(BF16)
 
-    pl.semaphore_wait(barrier, n - 1)
-    for j in far:
-        one_copy(j).start()
-    for q, r, j in peers:
-        ids_copy(q, r, j).start()
     big_all[0:cb, :] = big_send[0:cb, :]
 
     small_slot = jnp.where(is_big, -1, bucket * cs + rank)
@@ -162,12 +161,17 @@
         else:
             relay[0:span, :] = picked
             small_recv[0:cs, :] = picked[0:cs]
-        for j in far + [0]:
-            if r:
-                side_copy(r, j).start()
-            elif j:
-                line_copy(r, j).start()
-
+
+    pl.semaphore_wait(barrier, n - 1)
+    for j in steps:
+        one_copy(j).start()
+    for q, r, j in peers:
+        ids_copy(q, r, j).start()
+    for r in order:
+        for j in steps:
+            (side_copy if r else line_copy)(r, j).start()
+        if r:
+            side_copy(r, 0).start()
     for r in range(1, shards):
         if r == cores:
             for j in far:
@@ -175,7 +179,7 @@
             for r2 in range(1, shards):
                 if r2 == 1 or r2 % cores == 0:
                     two_copy(r2).start()
-        for j in far:
+        for j in steps:
             side_copy(r, j).wait_recv()
             line_copy(r, j).start()
 
@@ -187,7 +191,7 @@
     inside = (at >= low) & (at < low + cs)
     base = jnp.sum(jnp.where(inside, low, 0).astype(F32), axis=1, keepdims=True).astype(jnp.int32)
     small_lane = iota((total, LANES), 1) == iota((total, LANES), 0) - base
-    marks = jnp.dot(inside.astype(BF16), ids_recv[:, 0, :].astype(BF16), preferred_element_type=F32)
+    marks = jnp.dot(inside.astype(BF16), ids_recv[:, 0, 0:LANES].astype(BF16), preferred_element_type=F32)
     marks = jnp.where(small_lane, marks, 0.0)
     small_col = jnp.sum(marks, axis=1, keepdims=True)
     small_row = nt(jnp.ones((8, LANES), BF16), marks.astype(BF16))[0:1]
@@ -197,7 +201,7 @@
     at = iota((big_total, n), 0)
     inside = (at >= low) & (at < low + cb)
     base = jnp.sum(jnp.where(inside, low, 0).astype(F32), axis=1, keepdims=True).astype(jnp.int32)
-    marks = jnp.dot(inside.astype(BF16), ids_recv[:, 1, :].astype(BF16), preferred_element_type=F32)
+    marks = jnp.dot(inside.astype(BF16), ids_recv[:, 0, LANES:].astype(BF16), preferred_element_type=F32)
     big_marks[...] = jnp.where(iota((big_total, LANES), 1) == iota((big_total, LANES), 0) - base, marks, 0.0)
 
     my_row = nt(jnp.ones((8, LANES), BF16), big_marks[0:group, :].astype(BF16))[0:1]
@@ -213,34 +217,46 @@
         if r == 0:
             allowed = allowed & (iota((group, group), 0) != iota((group, group), 1))
         best = jnp.maximum(best, jnp.max(jnp.where(allowed, scores, -1.0), axis=0, keepdims=True))
-    low = iota((blocks, group), 0) * cb
-    at = iota((blocks, group), 1)
+    low = iota((up(blocks, 16), group), 0) * cb
+    at = iota((up(blocks, 16), group), 1)
     spread = jnp.where((at >= low) & (at < low + cb), best, 0.0)
     place = lax.rem(iota((group, LANES), 0), cb) == iota((group, LANES), 1)
     back = exact_dot(spread, place.astype(F32))
     for b in range(blocks):
-        back_send[n + b] = jnp.broadcast_to(back[b : b + 1], (8, LANES))
+        back_send[n + b] = back[b : b + 1]
     for j in far:
         bback_copy(j).start()
     back_recv[n] = back_send[n]
 
-    for q, r, j in peers:
-        (line_copy if j else side_copy)(r, j).wait_recv()
+    def small_best(r0, r1, c0, c1):
+        scores = nt(small_recv[r0:r1, :], small_recv[c0:c1, :])
+        allowed = small_col[r0:r1] == small_row[:, c0:c1]
+        if r0 < c1 and c0 < r1:
+            allowed = allowed & (iota((r1 - r0, c1 - c0), 0) + r0 != iota((r1 - r0, c1 - c0), 1) + c0)
+        return jnp.max(jnp.where(allowed, scores, -1.0), axis=0, keepdims=True)
+
     width = next(w for w in (256, 128, total) if total % w == 0)
+    cut = total - span
     parts = []
-    for start in range(0, total, width):
-        scores = nt(small_recv[...], small_recv[start : start + width, :])
-        allowed = (small_col == small_row[:, start : start + width]) & (
-            iota((total, width), 0) != iota((total, width), 1) + start
-        )
-        parts.append(jnp.max(jnp.where(allowed, scores, -1.0), axis=0, keepdims=True))
+    for r in range(shards):
+        if r == shards - 1:
+            parts = [small_best(0, cut, c, c + width) for c in range(0, cut - width + 1, width)]
+        for j in range(blocks):
+            if (r, j) != (0, 0):
+                (line_copy if j else side_copy)(r, j).wait_recv()
+    for c in range(0, total, width):
+        late = small_best(cut, total, c, c + width)
+        if c // width < len(parts):
+            parts[c // width] = jnp.maximum(parts[c // width], late)
+        else:
+            parts.append(jnp.maximum(small_best(0, cut, c, c + width), late))
     best = jnp.concatenate(parts, axis=1) if len(parts) > 1 else parts[0]
     low = iota((n, total), 0) * cs
     at = iota((n, total), 1)
     spread = jnp.where((at >= low) & (at < low + cs), best, 0.0)
     back = exact_dot(spread, small_lane.astype(F32))
     for q in range(n):
-        back_send[q] = jnp.broadcast_to(back[q : q + 1], (8, LANES))
+        back_send[q] = back[q : q + 1]
     for q, r, j in peers:
         sback_copy(q, r, j).start()
     back_recv[0] = back_send[0]
@@ -298,11 +314,11 @@
                 pltpu.VMEM((n * cs, feature), BF16),
                 pltpu.VMEM((blocks * cb, feature), BF16),
                 pltpu.VMEM((n * cb, feature), BF16),
-                pltpu.VMEM((n, 8, LANES), F32),
-                pltpu.VMEM((n, 8, LANES), F32),
+                pltpu.VMEM((n, 1, 2 * LANES), F32),
+                pltpu.VMEM((n, 1, 2 * LANES), F32),
                 pltpu.VMEM((n * cb, LANES), F32),
-                pltpu.VMEM((n + blocks, 8, LANES), F32),
-                pltpu.VMEM((nb, 8, LANES), F32),
+                pltpu.VMEM((n + blocks, 1, LANES), F32),
+                pltpu.VMEM((nb, 1, LANES), F32),
                 dma((2,)), dma((n,)), dma((n,)), dma((n,)), dma((n,)), dma((n,)), dma((n,)), dma((blocks,)), dma((blocks,)),
                 dma((shards,)), dma((shards,)), dma((n,)), dma((n,)), dma((blocks,)), dma((blocks,)),
             ],
@@ -310,7 +326,7 @@
                 collective_id=0, has_side_effects=True, vmem_limit_bytes=60 * 1024 * 1024
             ),
         )(pooled, proj_weight, cluster.reshape(1, rows))
-        return out.reshape(rows)
+        return jnp.maximum(out.reshape(rows), -1.0)
 
     in_specs = (P(("slab", "docs", "blk"), None), P(), P(("slab", "docs", "blk")))
     out_specs = P(("slab", "docs", "blk"))

time: 52.8 us -> 51.1 us (0.968)
  Pallas kernels: 51.4 us -> 49.7 us
  other arithmetic: 0 us -> 1.26 us
  local copies, waits for them, and re-layouts: 1.26 us -> 0 us
    pallas_call x1, Pallas kernels: 51.4 us -> 49.7 us  [body(): pl.pallas_call(functools.partial(kernel, (shards, blocks, cs, cb)), out_s...]
    max x0 -> x1, other arithmetic: none -> 1.26 us  [body(): return jnp.maximum(out.reshape(rows), -1.0)]
    unnamed x1 -> x0, local copies, waits for them, and re-layouts: 1.26 us -> none
where the time goes in v3:
time: 51.1 us; the launch traced here: 50.9 us
  Pallas kernels  49.7 us (97%)
  other arithmetic  1.26 us (2%)
    pallas_call x1, Pallas kernels, body(): pl.pallas_call(functools.partial(kernel, (shards, blocks, cs, cb)), out_s...  49.7 us
    max x1, other arithmetic, body(): return jnp.maximum(out.reshape(rows), -1.0)  1.26 us

profile of v3, /device:TPU:0, one launch (start us, length us, event | category | flops | bytes accessed | tf_op | source)
XLA Modules:
  0.0 50.9 jit_solution(5065202717399143992)
XLA Ops:
  0.0 49.7 %shard_map.37 = f32[1,512]{1,0:T(1,128)} custom-call(bf16[512,768]{1,0:T(8,128)(2,1)} %pooled_hbm.1, bf16[768,768]{1,0:T(8,128)(2,1)} %weight_hbm.1, s32[1,512]{1,0:T(1,128)} %bitcast.2), custom_call_target="tpu_custom_call" | custom-call | tf_op jit(solution)/shard_map/pallas_call | solution.py:299
  49.7 1.3 %broadcast_maximum_fusion = f32[1,512]{1,0:T(1,128)} fusion(f32[1,512]{1,0:T(1,128)} %shard_map.37), kind=kLoop, calls=%fused_computation | loop fusion | flops 512 | bytes 4096 | tf_op jit(solution)/shard_map/max | solution.py:329

commit v4 on v3

--- a/solution.py
+++ b/solution.py
@@ -173,7 +173,7 @@
         if r:
             side_copy(r, 0).start()
     for r in range(1, shards):
-        if r == cores:
+        if r == shards - 1:
             for j in far:
                 one_copy(j).wait_recv()
             for r2 in range(1, shards):

time: 51.1 us -> 51.1 us (level)
  no operation moved by 1% of the time
where the time goes in v4:
time: 51.1 us; the launch traced here: 50.9 us
  Pallas kernels  49.7 us (97%)
  other arithmetic  1.26 us (2%)
    pallas_call x1, Pallas kernels, body(): pl.pallas_call(functools.partial(kernel, (shards, blocks, cs, cb)), out_s...  49.7 us
    max x1, other arithmetic, body(): return jnp.maximum(out.reshape(rows), -1.0)  1.26 us

profile of v4, /device:TPU:0, one launch (start us, length us, event | category | flops | bytes accessed | tf_op | source)
XLA Modules:
  0.0 50.9 jit_solution(9636242917484935394)
XLA Ops:
  0.0 49.7 %shard_map.37 = f32[1,512]{1,0:T(1,128)} custom-call(bf16[512,768]{1,0:T(8,128)(2,1)} %pooled_hbm.1, bf16[768,768]{1,0:T(8,128)(2,1)} %weight_hbm.1, s32[1,512]{1,0:T(1,128)} %bitcast.2), custom_call_target="tpu_custom_call" | custom-call | tf_op jit(solution)/shard_map/pallas_call | solution.py:299
  49.7 1.3 %broadcast_maximum_fusion = f32[1,512]{1,0:T(1,128)} fusion(f32[1,512]{1,0:T(1,128)} %shard_map.37), kind=kLoop, calls=%fused_computation | loop fusion | flops 512 | bytes 4096 | tf_op jit(solution)/shard_map/max | solution.py:329
